TPU v7x, 32 devices: a whole 2x2x4 slice. The times are simulated.
32 devices in a mesh: chan: 4 (over x, core), rad: 8 (over z, y).
Axes of the slice: x: 2, y: 2, z: 4, core: 2. Of those that a mesh axis runs over, the one named last changes fastest.
Arguments:
- psi: float32 [2, 768, 128, 128], P(None, 'chan', 'rad'), may hold values from -6 to 6
- k_prev: float32 [2, 768, 128, 128], P(None, 'chan', 'rad'), may hold values from -6 to 6
- gaunt: bfloat16 [4, 768, 768], replicated, may hold values from -0.875 to 0.875
- dipole: bfloat16 [768, 768], replicated, may hold values from -0.875 to 0.875
- kinetic: float32 [128, 128], replicated, as said below
- chan_l: int32 [768, 2], P('chan'), may hold values from 0 to 23
- field_amp: float32 [1], replicated, may hold values from 0.02 to 0.1
Outputs:
- deriv: float32 [2, 768, 128, 128], P(None, 'chan', 'rad')
Inputs may be any that keep to these rules, and one draw needn't show every extreme that they name: `kinetic`: symmetric; zero where the row's and the column's blocks of 16 indices are more than one block apart.
All inputs are finite; a program needn't handle non-finite values.
Results may differ from a plain program's by a relative error of at most 0.00037.
Values may be sent and summed in bfloat16 or wider, within the bound.
A program may use at most 64 MiB of HBM per device.

v0:
```python
import jax
import jax.numpy as jnp
from jax import lax
from jax.sharding import PartitionSpec as P


def extended(array, sides, width):
    for axis, dim in sides:
        peers, length = (lax.axis_size(axis), array.shape[dim])
        up = [(i, (i + 1) % peers) for i in range(peers - 1)]
        down = [(j, i) for i, j in up]
        last = lax.slice_in_dim(array, length - width, length, axis=dim)
        initial = lax.slice_in_dim(array, 0, width, axis=dim)
        before = lax.ppermute(last, axis, up)
        after = lax.ppermute(initial, axis, down)
        array = jnp.concatenate([before, array, after], axis=dim)
    return array


def on_device(psi, k_prev, gaunt, dipole, kinetic, chan_l, field_amp):
    highest = lax.Precision.HIGHEST
    section = psi + 0.5 * k_prev
    local_chan = section.shape[1]
    rows = section.shape[2]
    width = section.shape[3]
    rad_at = lax.axis_index("rad")
    first_r = (
        1.0 + 8.0 * (rad_at * rows + jnp.arange(rows, dtype=jnp.int32)).astype(jnp.float32) / width
    )
    second_r = 1.0 + 8.0 * jnp.arange(width, dtype=jnp.float32) / width
    along_r2 = jnp.einsum("acij,kj->acik", section, kinetic, precision=highest)
    padded = extended(section.astype(jnp.bfloat16), (("rad", 2),), rows).astype(section.dtype)
    band = lax.dynamic_slice_in_dim(kinetic, rad_at * rows, rows, 0)
    widened = jnp.pad(band, ((0, 0), (rows, rows)))
    local_band = lax.dynamic_slice_in_dim(widened, rad_at * rows, 3 * rows, 1)
    along_r1 = jnp.einsum("ij,acjk->acik", local_band, padded, precision=highest)
    lvals = chan_l.astype(jnp.float32)
    first_l = lvals[:, 0] * (lvals[:, 0] + 1.0)
    second_l = lvals[:, 1] * (lvals[:, 1] + 1.0)
    potential = (
        first_l[:, None, None] / (2.0 * first_r * first_r)[None, :, None]
        + second_l[:, None, None] / (2.0 * second_r * second_r)[None, None, :]
        - 2.0 / first_r[None, :, None]
        - 2.0 / second_r[None, None, :]
    )
    sent = section.astype(jnp.bfloat16).reshape(2, local_chan, rows * width)
    chan_at = lax.axis_index("chan")
    block = lax.all_to_all(sent, "chan", split_axis=2, concat_axis=1, tiled=True)
    count = block.shape[2]
    place = chan_at * count + jnp.arange(count, dtype=jnp.int32)
    row_r = 1.0 + 8.0 * (rad_at * rows + place // width).astype(jnp.float32) / width
    col_r = 1.0 + 8.0 * (place % width).astype(jnp.float32) / width
    far = jnp.maximum(row_r, col_r)
    near = jnp.minimum(row_r, col_r)
    inverse = 1.0 / far
    ratio = near * inverse
    power = inverse
    total = jnp.zeros(block.shape, jnp.float32)
    for order in range(gaunt.shape[0]):
        mixed = jnp.einsum("cd,adq->acq", gaunt[order], block, preferred_element_type=jnp.float32)
        total = total + power[None, None, :] * mixed
        power = power * ratio
    mixed = jnp.einsum("cd,adq->acq", dipole, block, preferred_element_type=jnp.float32)
    total = total + (field_amp[0] * (row_r + col_r))[None, None, :] * mixed
    coupled = lax.all_to_all(
        total.astype(jnp.bfloat16), "chan", split_axis=1, concat_axis=2, tiled=True
    )
    coupled = coupled.reshape(coupled.shape[0], local_chan, rows, width)
    ham = along_r1 + along_r2 + potential[None] * section + coupled.astype(jnp.float32)
    return jnp.stack([ham[1], -ham[0]])


def solution(mesh):
    placed = (
        P(None, "chan", "rad", None),
        P(None, "chan", "rad", None),
        P(),
        P(),
        P(),
        P("chan", None),
        P(),
    )
    return jax.shard_map(
        on_device,
        mesh=mesh,
        in_specs=placed,
        out_specs=P(None, "chan", "rad", None),
        check_vma=False,
    )
```

profile of v0, /device:TPU:0, one launch (start us, length us, event | category | flops | bytes accessed | tf_op | source)
XLA Modules:
  0.0 111.4 jit_solution(17644316627872621807)
XLA Ops:
  0.0 0.0 copy-start
  0.0 4.5 %fusion.45 = bf16[2,192,16,128]{3,2,1,0:T(8,128)(2,1)} fusion(f32[2,192,16,128]{3,2,1,0:T(8,128)} %param.7, f32[2,192,16,128]{3,2,1,0:T(8,128)} %param.8), kind=kLoop, calls=%fused_computation.70 | loop fusion | flops 2359296 | bytes 7864320 | tf_op jit(solution)/shard_map/convert_element_type | solution.py:32
  4.5 0.0 copy-start.2
  4.5 0.0 copy-start.1
  4.5 6.2 %collective-permute-start = (bf16[2,192,16,128]{3,2,1,0:T(8,128)(2,1)}, bf16[2,192,16,128]{3,2,1,0:T(8,128)(2,1)}, u32[]{:S(2)}, u32[]{:S(2)}) collective-permute-start(bf16[2,192,16,128]{3,2,1,0:T(8,128)(2,1)} %fusion.45), channel_id=1, source_target_pairs={{0,1},{1,2},{2,3},{3,4},{4,5},{5,6},{6,7},{8,9},{9,10},{10,11},{11... | collective-permute-start | bytes 4718600 | tf_op jit(solution)/shard_map/ppermute | solution.py:14
  10.7 1.3 %collective-permute-start.1 = (bf16[2,192,16,128]{3,2,1,0:T(8,128)(2,1)}, bf16[2,192,16,128]{3,2,1,0:T(8,128)(2,1)}, u32[]{:S(2)}, u32[]{:S(2)}) collective-permute-start(bf16[2,192,16,128]{3,2,1,0:T(8,128)(2,1)} %fusion.45), channel_id=1, source_target_pairs={{1,0},{2,1},{3,2},{4,3},{5,4},{6,5},{7,6},{9,8},{10,9},{11,10},{12... | collective-permute-start | bytes 4718600 | tf_op jit(solution)/shard_map/ppermute | solution.py:15
  12.0 4.6 %copy.43 = bf16[2,192,16,128]{1,0,3,2:T(2,128)(2,1)} copy(bf16[2,192,16,128]{3,2,1,0:T(8,128)(2,1)} %fusion.45) | data formatting | bytes 3145728 | tf_op jit(solution)/shard_map/reshape | solution.py:46
  16.6 3.6 %all-to-all-start = ((bf16[2,192,2048]{1,0,2:T(2,128)(2,1)}), bf16[2,192,2048]{1,0,2:T(2,128)(2,1)S(1)}, u32[]{:S(2)}, u32[]{:S(2)}) async-start(bf16[2,192,2048]{1,0,2:T(2,128)(2,1)} %bitcast.55), calls=%async_computation | async-start | bytes 4194304 | tf_op jit(solution)/shard_map/all_to_all | solution.py:48
  20.9 0.0 copy-done.2
  21.0 0.0 copy-done.1
  21.1 0.1 broadcast_divide_fusion.1
  21.2 24.7 %all-to-all-done = bf16[2,192,2048]{1,0,2:T(2,128)(2,1)S(1)} async-done(((bf16[2,192,2048]{1,0,2:T(2,128)(2,1)}), bf16[2,192,2048]{1,0,2:T(2,128)(2,1)S(1)}, u32[]{:S(2)}, u32[]{:S(2)}) %all-to-all-start) | async-done | bytes 1572896 | tf_op jit(solution)/shard_map/all_to_all | solution.py:48
  45.8 4.6 %copy.44 = bf16[2,192,4,512]{3,2,1,0:T(4,128)(2,1)} copy(bf16[2,192,4,512]{1,0,3,2:T(2,128)(2,1)S(1)} %bitcast.54) | data formatting | bytes 3145728 | tf_op jit(solution)/shard_map/all_to_all | solution.py:48
  50.5 0.0 slice-start
  50.5 1.9 %copy.27 = bf16[2,4,192,512]{3,2,1,0:T(8,128)(2,1)S(1)} copy(bf16[2,4,192,512]{3,1,2,0:T(4,128)(2,1)} %bitcast.56) | data formatting | bytes 3145728 | tf_op jit(solution)/shard_map/all_to_all | solution.py:48
  52.4 0.0 slice-start.1
  52.4 2.8 %fusion.12 = f32[2,512,768]{2,1,0:T(8,128)S(1)} fusion(bf16[2,768,512]{2,1,0:T(8,128)(2,1)S(1)} %bitcast.58, bf16[4,768,768]{2,1,0:T(8,128)(2,1)} %param.9), kind=kOutput, calls=%fused_computation.17 | convolution fusion | flops 1207959552 | bytes 5898240 | tf_op jit(solution)/shard_map/cd,adq->acq/dot_general | solution.py:60
  55.1 2.7 %fusion.14 = f32[2,512,768]{2,1,0:T(8,128)S(1)} fusion(bf16[2,768,512]{2,1,0:T(8,128)(2,1)S(1)} %bitcast.59, bf16[4,768,768]{2,1,0:T(8,128)(2,1)} %param.9), kind=kOutput, calls=%fused_computation.19 | convolution fusion | flops 1207959552 | bytes 5898240 | tf_op jit(solution)/shard_map/cd,adq->acq/dot_general | solution.py:60
  57.8 0.0 slice-done
  57.9 0.0 slice-done.1
  57.9 1.4 %fusion.16 = f32[2,512,768]{2,1,0:T(8,128)S(1)} fusion(bf16[2,768,512]{2,1,0:T(8,128)(2,1)S(1)} %bitcast.60, bf16[4,768,768]{2,1,0:T(8,128)(2,1)S(1)} %bitcast.66), kind=kOutput, calls=%fused_computation.21 | convolution fusion | flops 1207959552 | bytes 5898240 | tf_op jit(solution)/shard_map/cd,adq->acq/dot_general | solution.py:60
  59.3 1.4 %fusion.18 = f32[2,512,768]{2,1,0:T(8,128)S(1)} fusion(bf16[2,768,512]{2,1,0:T(8,128)(2,1)S(1)} %bitcast.61, bf16[4,768,768]{2,1,0:T(8,128)(2,1)S(1)} %bitcast.66), kind=kOutput, calls=%fused_computation.23 | convolution fusion | flops 1207959552 | bytes 5898240 | tf_op jit(solution)/shard_map/cd,adq->acq/dot_general | solution.py:60
  60.8 0.0 copy-done
  60.8 2.7 %fusion.10 = bf16[2,768,512]{1,2,0:T(8,128)(2,1)S(1)} fusion(bf16[2,768,512]{2,1,0:T(8,128)(2,1)S(1)} %bitcast.62, f32[512]{0:T(512)S(1)} %get-tuple-element.9, f32[2,512,768]{2,1,0:T(8,128)S(1)} %fusion.12, f32[512]{0:T(512)S(1)} %get-tuple-element.12, f32[2,512,768]{2,1,0:T(8,128)S(1)} %fusion.14, f32[512]{0:T(512)S(1)} %fusion.40, ...), kind=kOutput, calls=%fused_computation.15 | convolution fusion | flops 1215823872 | bytes 16918528 | tf_op jit(solution)/shard_map/cd,adq->acq/dot_general | solution.py:63
  63.4 3.0 %copy.33 = bf16[2,768,512]{2,0,1:T(2,128)(2,1)} copy(bf16[2,768,512]{1,2,0:T(8,128)(2,1)S(1)} %fusion.10) | data formatting | bytes 3145728 | tf_op jit(solution)/shard_map/convert_element_type | solution.py:66
  66.5 4.5 %all-to-all-start.1 = ((bf16[2,768,512]{2,0,1:T(2,128)(2,1)}), bf16[2,768,512]{2,0,1:T(2,128)(2,1)}, u32[]{:S(2)}, u32[]{:S(2)}) async-start(bf16[2,768,512]{2,0,1:T(2,128)(2,1)} %copy.33), calls=%async_computation.1 | async-start | bytes 3145728 | tf_op jit(solution)/shard_map/all_to_all | solution.py:65
  71.0 0.1 broadcast_divide_fusion
  71.1 0.5 subtract_subtract_fusion
  71.6 5.9 %fusion.24 = f32[2,192,16,128]{3,2,1,0:T(8,128)} fusion(f32[128,128]{1,0:T(8,128)S(1)} %copy-done.1, f32[2,192,16,128]{3,2,1,0:T(8,128)} %param.7, f32[2,192,16,128]{3,2,1,0:T(8,128)} %param.8), kind=kOutput, calls=%fused_computation.29 | convolution fusion | flops 1209532416 | bytes 9502720 | tf_op jit(solution)/shard_map/acij,kj->acik/dot_general | solution.py:31
  77.5 13.5 %all-to-all-done.1 = bf16[2,768,512]{2,0,1:T(2,128)(2,1)} async-done(((bf16[2,768,512]{2,0,1:T(2,128)(2,1)}), bf16[2,768,512]{2,0,1:T(2,128)(2,1)}, u32[]{:S(2)}, u32[]{:S(2)}) %all-to-all-start.1) | async-done | bytes 1572896 | tf_op jit(solution)/shard_map/all_to_all | solution.py:65
  90.9 1.7 %copy.34 = bf16[2,768,512]{2,1,0:T(8,128)(2,1)S(1)} copy(bf16[2,768,512]{2,0,1:T(2,128)(2,1)} %all-to-all-done.1) | data formatting | bytes 3145728 | tf_op jit(solution)/shard_map/all_to_all | solution.py:65
  92.6 0.4 convert_bitcast_fusion
  93.0 3.7 %copy.35 = f32[2,192,4,512]{3,2,1,0:T(4,128)} copy(f32[2,192,4,512]{3,1,2,0:T(8,128)S(1)} %convert_bitcast_fusion) | data formatting | bytes 6291456 | tf_op jit(solution)/shard_map/convert_element_type | solution.py:69
  96.7 5.1 %reshape.171 = f32[2,192,16,128]{3,2,1,0:T(8,128)} reshape(f32[2,192,4,512]{3,2,1,0:T(4,128)} %copy.35) | data formatting | bytes 6291456 | tf_op jit(solution)/shard_map/convert_element_type | solution.py:69
  101.8 0.0 copy-start.3
  101.8 0.0 collective-permute-done
  101.8 0.0 collective-permute-done.1
  101.8 7.6 %fusion.7 = f32[2,192,16,128]{3,2,1,0:T(8,128)S(1)} fusion(f32[2,192,16,128]{3,2,1,0:T(8,128)} %reshape.171, f32[2,192,16,128]{3,2,1,0:T(8,128)} %fusion.24, bf16[2,192,16,128]{3,2,1,0:T(8,128)(2,1)} %collective-permute-done.1, bf16[2,192,16,128]{3,2,1,0:T(8,128)(2,1)} %fusion.45, bf16[2,192,16,128]{3,2,1,0:T(8,128)(2,1)} %collective-permute-done, ...), kind=kOutput, calls=%fused_computation.10 | convolution fusion | flops 471859200 | bytes 22028292 | tf_op jit(solution)/shard_map/ij,acjk->acik/dot_general | solution.py:36
  109.4 0.0 copy-done.3
  109.4 0.3 fusion.46
  109.7 0.0 copy-start.4
  109.7 1.7 %copy-done.4 = f32[2,192,16,128]{3,2,1,0:T(8,128)} copy-done((f32[2,192,16,128]{3,2,1,0:T(8,128)}, f32[2,192,16,128]{3,2,1,0:T(8,128)S(1)}, u32[]{:S(2)}) %copy-start.4) | copy-done | bytes 3145752
  (14 shorter events, 0.1 us)
Async XLA Ops:
  0.0 60.8 %copy-start = (bf16[768,768]{1,0:T(8,128)(2,1)S(1)}, bf16[768,768]{1,0:T(8,128)(2,1)}, u32[]{:S(2)}) copy-start(bf16[768,768]{1,0:T(8,128)(2,1)} %param.10) | copy-start | bytes 3538948
  4.5 16.4 %copy-start.2 = (s32[192,2]{0,1:T(2,128)S(1)}, s32[192,2]{0,1:T(2,128)}, u32[]{:S(2)}) copy-start(s32[192,2]{0,1:T(2,128)} %param.12) | copy-start | bytes 4612
  4.5 16.5 %copy-start.1 = (f32[128,128]{1,0:T(8,128)S(1)}, f32[128,128]{1,0:T(8,128)}, u32[]{:S(2)}) copy-start(f32[128,128]{1,0:T(8,128)} %param.11) | copy-start | bytes 196612
  4.5 97.3 %collective-permute-start = (bf16[2,192,16,128]{3,2,1,0:T(8,128)(2,1)}, bf16[2,192,16,128]{3,2,1,0:T(8,128)(2,1)}, u32[]{:S(2)}, u32[]{:S(2)}) collective-permute-start(bf16[2,192,16,128]{3,2,1,0:T(8,128)(2,1)} %fusion.45), channel_id=1, source_target_pairs={{0,1},{1,2},{2,3},{3,4},{4,5},{5,6},{6,7},{8,9},{9,10},{10,11},{11... | collective-permute-start | bytes 4718600 | tf_op jit(solution)/shard_map/ppermute | solution.py:14
  10.7 91.1 %collective-permute-start.1 = (bf16[2,192,16,128]{3,2,1,0:T(8,128)(2,1)}, bf16[2,192,16,128]{3,2,1,0:T(8,128)(2,1)}, u32[]{:S(2)}, u32[]{:S(2)}) collective-permute-start(bf16[2,192,16,128]{3,2,1,0:T(8,128)(2,1)} %fusion.45), channel_id=1, source_target_pairs={{1,0},{2,1},{3,2},{4,3},{5,4},{6,5},{7,6},{9,8},{10,9},{11,10},{12... | collective-permute-start | bytes 4718600 | tf_op jit(solution)/shard_map/ppermute | solution.py:15
  16.6 29.2 %all-to-all-start = ((bf16[2,192,2048]{1,0,2:T(2,128)(2,1)}), bf16[2,192,2048]{1,0,2:T(2,128)(2,1)S(1)}, u32[]{:S(2)}, u32[]{:S(2)}) async-start(bf16[2,192,2048]{1,0,2:T(2,128)(2,1)} %bitcast.55), calls=%async_computation | async-start | bytes 4194304 | tf_op jit(solution)/shard_map/all_to_all | solution.py:48
  50.5 7.4 %slice-start = ((s8[4718592]{0:T(1024)(128)(4,1)}), s8[4194304]{0:T(1024)(128)(4,1)S(1)}, s32[]{:S(2)}) async-start(s8[4718592]{0:T(1024)(128)(4,1)} %bitcast.65), calls=%async_computation.2 | async-start | bytes 8388608
  52.4 5.5 %slice-start.1 = ((s8[4718592]{0:T(1024)(128)(4,1)}), s8[524288]{0:T(1024)(128)(4,1)S(1)}, s32[]{:S(2)}) async-start(s8[4718592]{0:T(1024)(128)(4,1)} %bitcast.65), calls=%async_computation.3 | async-start | bytes 1048576
  66.5 24.5 %all-to-all-start.1 = ((bf16[2,768,512]{2,0,1:T(2,128)(2,1)}), bf16[2,768,512]{2,0,1:T(2,128)(2,1)}, u32[]{:S(2)}, u32[]{:S(2)}) async-start(bf16[2,768,512]{2,0,1:T(2,128)(2,1)} %copy.33), calls=%async_computation.1 | async-start | bytes 3145728 | tf_op jit(solution)/shard_map/all_to_all | solution.py:65
  101.8 7.6 %copy-start.3 = (f32[2,192,16,128]{3,2,1,0:T(8,128)S(1)}, f32[2,192,16,128]{3,2,1,0:T(8,128)}, u32[]{:S(2)}) copy-start(f32[2,192,16,128]{3,2,1,0:T(8,128)} %custom-call) | copy-start | bytes 9437188
  109.7 1.7 %copy-start.4 = (f32[2,192,16,128]{3,2,1,0:T(8,128)}, f32[2,192,16,128]{3,2,1,0:T(8,128)S(1)}, u32[]{:S(2)}) copy-start(f32[2,192,16,128]{3,2,1,0:T(8,128)S(1)} %get-tuple-element.17) | copy-start | bytes 9437188
where the time goes:
time: 112 us; the launch traced here: 111 us
  waiting for transfers between devices  38.1 us (34%)
  local copies, waits for them, and re-layouts  26.3 us (23%)
  matrix products  24.4 us (22%)
  starting transfers between devices  15.6 us (14%)
  other arithmetic  5.95 us (5%)
    all_to_all x1, waiting for transfers between devices, on_device(): lax.all_to_all(sent, 'chan', split_axis=2, concat_axis=1, tiled=True)  24.7 us
    all_to_all x1, waiting for transfers between devices, on_device(): lax.all_to_all(total.astype(jnp.bfloat16), 'chan', split_axis=1, concat_a...  13.5 us
    convert_element_type x2, local copies, waits for them, and re-layouts, on_device(): coupled.astype(jnp.float32)  8.79 us
    dot_general x4, matrix products, on_device(): jnp.einsum('cd,adq->acq', gaunt[order], block, preferred_element_type=jnp...  8.34 us
    dot_general x1, matrix products, on_device(): jnp.einsum('ij,acjk->acik', local_band, padded, precision=highest)  7.55 us
    all_to_all x2, local copies, waits for them, and re-layouts, on_device(): lax.all_to_all(sent, 'chan', split_axis=2, concat_axis=1, tiled=True)  6.5 us
    ppermute x1, starting transfers between devices, extended(): before = lax.ppermute(last, axis, up)  6.2 us
    dot_general x1, matrix products, on_device(): along_r2 = jnp.einsum('acij,kj->acik', section, kinetic, precision=highest)  5.87 us
  transfers between devices with their start and end apart: 4, of which 2 were waited for; matrix products, arithmetic and copies ran while one was open for 38% of the time, Pallas kernels for 0%

commit v1 on v0

--- a/solution.py
+++ b/solution.py
@@ -45,7 +45,10 @@
     )
     sent = section.astype(jnp.bfloat16).reshape(2, local_chan, rows * width)
     chan_at = lax.axis_index("chan")
-    block = lax.all_to_all(sent, "chan", split_axis=2, concat_axis=1, tiled=True)
+    block = jnp.concatenate(
+        lax.all_to_all(jnp.stack(jnp.split(sent, lax.axis_size("chan"), axis=2)), "chan", 0, 0),
+        axis=1,
+    )
     count = block.shape[2]
     place = chan_at * count + jnp.arange(count, dtype=jnp.int32)
     row_r = 1.0 + 8.0 * (rad_at * rows + place // width).astype(jnp.float32) / width

time: 112 us -> 99.3 us (0.89)
  local copies, waits for them, and re-layouts: 26.3 us -> 18 us
  waiting for transfers between devices: 38.1 us -> 32.5 us
  other arithmetic: 5.95 us -> 7.28 us
    all_to_all x2 -> x1, local copies, waits for them, and re-layouts: 6.5 us -> 0.16 us  [on_device(): lax.all_to_all(jnp.stack(jnp.split(sent, lax.axis_size('chan'), axis=2)),...]
    all_to_all x1, waiting for transfers between devices: 24.7 us -> 19 us  [on_device(): lax.all_to_all(jnp.stack(jnp.split(sent, lax.axis_size('chan'), axis=2)),...]
    reshape x1, local copies, waits for them, and re-layouts: 4.61 us -> 2.55 us  [on_device(): sent = section.astype(jnp.bfloat16).reshape(2, local_chan, rows * width)]
    another operation x0 -> x1, other arithmetic: none -> 1.34 us  [on_device(): jnp.stack(jnp.split(sent, lax.axis_size('chan'), axis=2))]
  transfers between devices with their start and end apart: 4 -> 4, of which waited for: 2 -> 2; matrix products, arithmetic and copies ran while one was open for 38% -> 36% of each run, Pallas kernels for 0% -> 0%
where the time goes in v1:
time: 99.3 us; the launch traced here: 98.8 us
  waiting for transfers between devices  32.5 us (33%)
  matrix products  24.5 us (25%)
  local copies, waits for them, and re-layouts  18 us (18%)
  starting transfers between devices  15.5 us (16%)
  other arithmetic  7.28 us (7%)
    all_to_all x1, waiting for transfers between devices, on_device(): lax.all_to_all(jnp.stack(jnp.split(sent, lax.axis_size('chan'), axis=2)),...  19 us
    all_to_all x1, waiting for transfers between devices, on_device(): lax.all_to_all(total.astype(jnp.bfloat16), 'chan', split_axis=1, concat_a...  13.5 us
    convert_element_type x2, local copies, waits for them, and re-layouts, on_device(): coupled.astype(jnp.float32)  8.8 us
    dot_general x4, matrix products, on_device(): jnp.einsum('cd,adq->acq', gaunt[order], block, preferred_element_type=jnp...  8.43 us
    dot_general x1, matrix products, on_device(): jnp.einsum('ij,acjk->acik', local_band, padded, precision=highest)  7.55 us
    ppermute x1, starting transfers between devices, extended(): before = lax.ppermute(last, axis, up)  6.09 us
    dot_general x1, matrix products, on_device(): along_r2 = jnp.einsum('acij,kj->acik', section, kinetic, precision=highest)  5.88 us
    all_to_all x1, starting transfers between devices, on_device(): lax.all_to_all(total.astype(jnp.bfloat16), 'chan', split_axis=1, concat_a...  4.54 us
  transfers between devices with their start and end apart: 4, of which 2 were waited for; matrix products, arithmetic and copies ran while one was open for 36% of the time, Pallas kernels for 0%

profile of v1, /device:TPU:0, one launch (start us, length us, event | category | flops | bytes accessed | tf_op | source)
XLA Modules:
  0.0 98.8 jit_solution(9805092671252039075)
XLA Ops:
  0.0 0.0 copy-start
  0.0 4.5 %fusion.45 = bf16[2,192,16,128]{3,2,1,0:T(8,128)(2,1)} fusion(f32[2,192,16,128]{3,2,1,0:T(8,128)} %param.7, f32[2,192,16,128]{3,2,1,0:T(8,128)} %param.8), kind=kLoop, calls=%fused_computation.75 | loop fusion | flops 2359296 | bytes 7864320 | tf_op jit(solution)/shard_map/convert_element_type | solution.py:32
  4.5 6.1 %collective-permute-start = (bf16[2,192,16,128]{3,2,1,0:T(8,128)(2,1)}, bf16[2,192,16,128]{3,2,1,0:T(8,128)(2,1)}, u32[]{:S(2)}, u32[]{:S(2)}) collective-permute-start(bf16[2,192,16,128]{3,2,1,0:T(8,128)(2,1)} %fusion.45), channel_id=1, source_target_pairs={{0,1},{1,2},{2,3},{3,4},{4,5},{5,6},{6,7},{8,9},{9,10},{10,11},{11... | collective-permute-start | bytes 4718600 | tf_op jit(solution)/shard_map/ppermute | solution.py:14
  10.6 1.3 %collective-permute-start.1 = (bf16[2,192,16,128]{3,2,1,0:T(8,128)(2,1)}, bf16[2,192,16,128]{3,2,1,0:T(8,128)(2,1)}, u32[]{:S(2)}, u32[]{:S(2)}) collective-permute-start(bf16[2,192,16,128]{3,2,1,0:T(8,128)(2,1)} %fusion.45), channel_id=1, source_target_pairs={{1,0},{2,1},{3,2},{4,3},{5,4},{6,5},{7,6},{9,8},{10,9},{11,10},{12... | collective-permute-start | bytes 4718600 | tf_op jit(solution)/shard_map/ppermute | solution.py:15
  11.9 2.5 %reshape.176 = bf16[2,192,2048]{2,1,0:T(8,128)(2,1)S(1)} reshape(bf16[2,192,16,128]{3,2,1,0:T(8,128)(2,1)} %fusion.45) | data formatting | bytes 3145728 | tf_op jit(solution)/shard_map/reshape | solution.py:46
  14.4 0.1 slice_bitcast_fusion.3
  14.6 0.0 copy-start.2
  14.6 0.0 copy-start.1
  14.6 1.3 %pad_maximum_fusion.1 = bf16[4,2,192,512]{3,2,1,0:T(8,128)(2,1)} fusion(bf16[1,2,192,512]{3,2,1,0:T(8,128)(2,1)S(1)} %get-tuple-element.8, bf16[1,2,192,512]{3,2,1,0:T(8,128)(2,1)S(1)} %get-tuple-element.9, bf16[1,2,192,512]{3,2,1,0:T(8,128)(2,1)S(1)} %get-tuple-element.10, bf16[1,2,192,512]{3,2,1,0:T(8,128)(2,1)S(1)} %get-tuple-element.7), kind=kLoop, calls=%fused_computation.14 | loop fusion | flops 2359296 | bytes 3145728 | tf_op jit(solution)/shard_map/stack | solution.py:49
  15.9 3.6 %all-to-all-start = ((bf16[4,2,192,512]{3,2,1,0:T(8,128)(2,1)}), bf16[4,2,192,512]{3,2,1,0:T(8,128)(2,1)S(1)}, u32[]{:S(2)}, u32[]{:S(2)}) async-start(bf16[4,2,192,512]{3,2,1,0:T(8,128)(2,1)} %pad_maximum_fusion.1), calls=%async_computation | async-start | bytes 3145728 | tf_op jit(solution)/shard_map/all_to_all | solution.py:49
  20.2 0.0 copy-done.2
  20.3 0.0 copy-done.1
  20.4 0.1 broadcast_divide_fusion.1
  20.5 19.0 %all-to-all-done = bf16[4,2,192,512]{3,2,1,0:T(8,128)(2,1)S(1)} async-done(((bf16[4,2,192,512]{3,2,1,0:T(8,128)(2,1)}), bf16[4,2,192,512]{3,2,1,0:T(8,128)(2,1)S(1)}, u32[]{:S(2)}, u32[]{:S(2)}) %all-to-all-start) | async-done | bytes 1572896 | tf_op jit(solution)/shard_map/all_to_all | solution.py:49
  39.5 0.0 slice-start
  39.5 0.2 copy.20
  39.7 0.0 slice-start.1
  39.7 2.9 %fusion.12 = f32[2,512,768]{2,1,0:T(8,128)S(1)} fusion(bf16[2,768,512]{2,1,0:T(8,128)(2,1)S(1)} %bitcast.64, bf16[4,768,768]{2,1,0:T(8,128)(2,1)} %param.9), kind=kOutput, calls=%fused_computation.18 | convolution fusion | flops 1207959552 | bytes 5898240 | tf_op jit(solution)/shard_map/cd,adq->acq/dot_general | solution.py:63
  42.5 2.7 %fusion.14 = f32[2,512,768]{2,1,0:T(8,128)S(1)} fusion(bf16[2,768,512]{2,1,0:T(8,128)(2,1)S(1)} %bitcast.65, bf16[4,768,768]{2,1,0:T(8,128)(2,1)} %param.9), kind=kOutput, calls=%fused_computation.20 | convolution fusion | flops 1207959552 | bytes 5898240 | tf_op jit(solution)/shard_map/cd,adq->acq/dot_general | solution.py:63
  45.3 0.0 slice-done
  45.3 0.0 slice-done.1
  45.3 1.4 %fusion.16 = f32[2,512,768]{2,1,0:T(8,128)S(1)} fusion(bf16[2,768,512]{2,1,0:T(8,128)(2,1)S(1)} %bitcast.66, bf16[4,768,768]{2,1,0:T(8,128)(2,1)S(1)} %bitcast.72), kind=kOutput, calls=%fused_computation.22 | convolution fusion | flops 1207959552 | bytes 5898240 | tf_op jit(solution)/shard_map/cd,adq->acq/dot_general | solution.py:63
  46.7 1.4 %fusion.18 = f32[2,512,768]{2,1,0:T(8,128)S(1)} fusion(bf16[2,768,512]{2,1,0:T(8,128)(2,1)S(1)} %bitcast.67, bf16[4,768,768]{2,1,0:T(8,128)(2,1)S(1)} %bitcast.72), kind=kOutput, calls=%fused_computation.24 | convolution fusion | flops 1207959552 | bytes 5898240 | tf_op jit(solution)/shard_map/cd,adq->acq/dot_general | solution.py:63
  48.2 0.0 copy-done
  48.2 2.7 %fusion.10 = bf16[2,768,512]{1,2,0:T(8,128)(2,1)S(1)} fusion(bf16[2,768,512]{2,1,0:T(8,128)(2,1)S(1)} %bitcast.68, f32[512]{0:T(512)S(1)} %get-tuple-element.13, f32[2,512,768]{2,1,0:T(8,128)S(1)} %fusion.12, f32[512]{0:T(512)S(1)} %get-tuple-element.16, f32[2,512,768]{2,1,0:T(8,128)S(1)} %fusion.14, f32[512]{0:T(512)S(1)} %fusion.40, ...), kind=kOutput, calls=%fused_computation.16 | convolution fusion | flops 1215823872 | bytes 16918528 | tf_op jit(solution)/shard_map/cd,adq->acq/dot_general | solution.py:66
  50.8 3.0 %copy.26 = bf16[2,768,512]{2,0,1:T(2,128)(2,1)} copy(bf16[2,768,512]{1,2,0:T(8,128)(2,1)S(1)} %fusion.10) | data formatting | bytes 3145728 | tf_op jit(solution)/shard_map/convert_element_type | solution.py:69
  53.9 4.5 %all-to-all-start.1 = ((bf16[2,768,512]{2,0,1:T(2,128)(2,1)}), bf16[2,768,512]{2,0,1:T(2,128)(2,1)}, u32[]{:S(2)}, u32[]{:S(2)}) async-start(bf16[2,768,512]{2,0,1:T(2,128)(2,1)} %copy.26), calls=%async_computation.1 | async-start | bytes 3145728 | tf_op jit(solution)/shard_map/all_to_all | solution.py:68
  58.4 0.1 broadcast_divide_fusion
  58.5 0.5 subtract_subtract_fusion
  59.0 5.9 %fusion.24 = f32[2,192,16,128]{3,2,1,0:T(8,128)} fusion(f32[128,128]{1,0:T(8,128)S(1)} %copy-done.1, f32[2,192,16,128]{3,2,1,0:T(8,128)} %param.7, f32[2,192,16,128]{3,2,1,0:T(8,128)} %param.8), kind=kOutput, calls=%fused_computation.34 | convolution fusion | flops 1209532416 | bytes 9502720 | tf_op jit(solution)/shard_map/acij,kj->acik/dot_general | solution.py:31
  64.9 13.5 %all-to-all-done.1 = bf16[2,768,512]{2,0,1:T(2,128)(2,1)} async-done(((bf16[2,768,512]{2,0,1:T(2,128)(2,1)}), bf16[2,768,512]{2,0,1:T(2,128)(2,1)}, u32[]{:S(2)}, u32[]{:S(2)}) %all-to-all-start.1) | async-done | bytes 1572896 | tf_op jit(solution)/shard_map/all_to_all | solution.py:68
  78.3 1.7 %copy.27 = bf16[2,768,512]{2,1,0:T(8,128)(2,1)S(1)} copy(bf16[2,768,512]{2,0,1:T(2,128)(2,1)} %all-to-all-done.1) | data formatting | bytes 3145728 | tf_op jit(solution)/shard_map/all_to_all | solution.py:68
  80.0 0.4 convert_bitcast_fusion
  80.4 3.7 %copy.28 = f32[2,192,4,512]{3,2,1,0:T(4,128)} copy(f32[2,192,4,512]{3,1,2,0:T(8,128)S(1)} %convert_bitcast_fusion) | data formatting | bytes 6291456 | tf_op jit(solution)/shard_map/convert_element_type | solution.py:72
  84.1 5.1 %reshape.179 = f32[2,192,16,128]{3,2,1,0:T(8,128)} reshape(f32[2,192,4,512]{3,2,1,0:T(4,128)} %copy.28) | data formatting | bytes 6291456 | tf_op jit(solution)/shard_map/convert_element_type | solution.py:72
  89.2 0.0 copy-start.3
  89.2 0.0 collective-permute-done
  89.2 0.0 collective-permute-done.1
  89.3 7.6 %fusion.7 = f32[2,192,16,128]{3,2,1,0:T(8,128)S(1)} fusion(f32[2,192,16,128]{3,2,1,0:T(8,128)} %reshape.179, f32[2,192,16,128]{3,2,1,0:T(8,128)} %fusion.24, bf16[2,192,16,128]{3,2,1,0:T(8,128)(2,1)} %collective-permute-done.1, bf16[2,192,16,128]{3,2,1,0:T(8,128)(2,1)} %fusion.45, bf16[2,192,16,128]{3,2,1,0:T(8,128)(2,1)} %collective-permute-done, ...), kind=kOutput, calls=%fused_computation.10 | convolution fusion | flops 471859200 | bytes 22028292 | tf_op jit(solution)/shard_map/ij,acjk->acik/dot_general | solution.py:36
  96.8 0.0 copy-done.3
  96.8 0.3 fusion.46
  97.1 0.0 copy-start.4
  97.1 1.7 %copy-done.4 = f32[2,192,16,128]{3,2,1,0:T(8,128)} copy-done((f32[2,192,16,128]{3,2,1,0:T(8,128)}, f32[2,192,16,128]{3,2,1,0:T(8,128)S(1)}, u32[]{:S(2)}) %copy-start.4) | copy-done | bytes 3145752
  (14 shorter events, 0.1 us)
Async XLA Ops:
  0.0 48.2 %copy-start = (bf16[768,768]{1,0:T(8,128)(2,1)S(1)}, bf16[768,768]{1,0:T(8,128)(2,1)}, u32[]{:S(2)}) copy-start(bf16[768,768]{1,0:T(8,128)(2,1)} %param.10) | copy-start | bytes 3538948
  4.5 84.8 %collective-permute-start = (bf16[2,192,16,128]{3,2,1,0:T(8,128)(2,1)}, bf16[2,192,16,128]{3,2,1,0:T(8,128)(2,1)}, u32[]{:S(2)}, u32[]{:S(2)}) collective-permute-start(bf16[2,192,16,128]{3,2,1,0:T(8,128)(2,1)} %fusion.45), channel_id=1, source_target_pairs={{0,1},{1,2},{2,3},{3,4},{4,5},{5,6},{6,7},{8,9},{9,10},{10,11},{11... | collective-permute-start | bytes 4718600 | tf_op jit(solution)/shard_map/ppermute | solution.py:14
  10.6 78.7 %collective-permute-start.1 = (bf16[2,192,16,128]{3,2,1,0:T(8,128)(2,1)}, bf16[2,192,16,128]{3,2,1,0:T(8,128)(2,1)}, u32[]{:S(2)}, u32[]{:S(2)}) collective-permute-start(bf16[2,192,16,128]{3,2,1,0:T(8,128)(2,1)} %fusion.45), channel_id=1, source_target_pairs={{1,0},{2,1},{3,2},{4,3},{5,4},{6,5},{7,6},{9,8},{10,9},{11,10},{12... | collective-permute-start | bytes 4718600 | tf_op jit(solution)/shard_map/ppermute | solution.py:15
  14.6 5.6 %copy-start.2 = (s32[192,2]{0,1:T(2,128)S(1)}, s32[192,2]{0,1:T(2,128)}, u32[]{:S(2)}) copy-start(s32[192,2]{0,1:T(2,128)} %param.12) | copy-start | bytes 4612
  14.6 5.7 %copy-start.1 = (f32[128,128]{1,0:T(8,128)S(1)}, f32[128,128]{1,0:T(8,128)}, u32[]{:S(2)}) copy-start(f32[128,128]{1,0:T(8,128)} %param.11) | copy-start | bytes 196612
  15.9 23.6 %all-to-all-start = ((bf16[4,2,192,512]{3,2,1,0:T(8,128)(2,1)}), bf16[4,2,192,512]{3,2,1,0:T(8,128)(2,1)S(1)}, u32[]{:S(2)}, u32[]{:S(2)}) async-start(bf16[4,2,192,512]{3,2,1,0:T(8,128)(2,1)} %pad_maximum_fusion.1), calls=%async_computation | async-start | bytes 3145728 | tf_op jit(solution)/shard_map/all_to_all | solution.py:49
  39.5 5.8 %slice-start = ((s8[4718592]{0:T(1024)(128)(4,1)}), s8[4194304]{0:T(1024)(128)(4,1)S(1)}, s32[]{:S(2)}) async-start(s8[4718592]{0:T(1024)(128)(4,1)} %bitcast.71), calls=%async_computation.2 | async-start | bytes 8388608
  39.7 5.6 %slice-start.1 = ((s8[4718592]{0:T(1024)(128)(4,1)}), s8[524288]{0:T(1024)(128)(4,1)S(1)}, s32[]{:S(2)}) async-start(s8[4718592]{0:T(1024)(128)(4,1)} %bitcast.71), calls=%async_computation.3 | async-start | bytes 1048576
  53.9 24.5 %all-to-all-start.1 = ((bf16[2,768,512]{2,0,1:T(2,128)(2,1)}), bf16[2,768,512]{2,0,1:T(2,128)(2,1)}, u32[]{:S(2)}, u32[]{:S(2)}) async-start(bf16[2,768,512]{2,0,1:T(2,128)(2,1)} %copy.26), calls=%async_computation.1 | async-start | bytes 3145728 | tf_op jit(solution)/shard_map/all_to_all | solution.py:68
  89.2 7.6 %copy-start.3 = (f32[2,192,16,128]{3,2,1,0:T(8,128)S(1)}, f32[2,192,16,128]{3,2,1,0:T(8,128)}, u32[]{:S(2)}) copy-start(f32[2,192,16,128]{3,2,1,0:T(8,128)} %custom-call) | copy-start | bytes 9437188
  97.1 1.7 %copy-start.4 = (f32[2,192,16,128]{3,2,1,0:T(8,128)}, f32[2,192,16,128]{3,2,1,0:T(8,128)S(1)}, u32[]{:S(2)}) copy-start(f32[2,192,16,128]{3,2,1,0:T(8,128)S(1)} %get-tuple-element.21) | copy-start | bytes 9437188
